TPU v7x, 512 devices: a whole 4x4x16 slice. The times are simulated.
512 devices in a mesh: dst: 32 (over z, core), src: 16 (over y, x).
Axes of the slice: x: 4, y: 4, z: 16, core: 2. Of those that a mesh axis runs over, the one named last changes fastest.
Arguments:
- adj_tiles: bfloat16 [32, 16, 64, 64, 512], P('dst', 'src'), may hold values from 0 to 0.011047363
- tile_cols: int32 [32, 16, 64, 8], P('dst', 'src'), may hold values from 0 to 63
- send_block: int32 [32, 16, 32, 2], P('dst', 'src'), may hold values from 0 to 15
- send_count: int32 [32, 16, 32], P('dst', 'src'), may hold values from 1 to 2, as said below
- history: bfloat16 [64, 16, 8192], P('dst', 'src'), may hold values from -6 to 6
- node_feats: bfloat16 [512, 8192], P('dst', 'src'), may hold values from -6 to 6
- w_neigh: bfloat16 [128, 128], replicated, may hold values from -0.5 to 0.5
- w_self: bfloat16 [128, 128], replicated, may hold values from -0.5 to 0.5
- out_bias: float32 [128], replicated, may hold values from -3 to 3
- cotangent: bfloat16 [512, 8192], P('dst', 'src'), may hold values from -6 to 6
Outputs:
- new_embed: bfloat16 [512, 8192], P('dst', 'src')
- grad_neigh: float32 [128, 128], replicated
- grad_self: float32 [128, 128], replicated
- grad_bias: float32 [128], replicated
Inputs may be any that keep to these rules, and one draw needn't show every extreme that they name: `send_count`: in every draw, for each source group some owner gets 2 live slots from every device of that group.
All inputs are finite; a program needn't handle non-finite values.
Results may differ from a plain program's by a relative error of at most 0.0052.
Values may be sent and summed in bfloat16 or wider, within the bound.
A program may use at most 64 MiB of HBM per device.

v0:
```python
import jax
import jax.numpy as jnp
from jax import lax
from jax.sharding import PartitionSpec as P


def on_device(
    adj_tiles,
    tile_cols,
    send_block,
    send_count,
    history,
    node_feats,
    w_neigh,
    w_self,
    out_bias,
    cotangent,
):
    owners = lax.axis_size("dst")
    groups = lax.axis_size("src")
    slot_count = adj_tiles.shape[2]
    block_size = adj_tiles.shape[3]
    feat_width = w_neigh.shape[0]
    capacity = slot_count // owners
    own_blocks = node_feats.shape[0]
    gathered = lax.all_gather(history, "dst", axis=0, tiled=True)
    group_table = gathered.reshape(-1, block_size, feat_width)
    picked = group_table[tile_cols.reshape(-1)].reshape(slot_count, -1, feat_width)
    tiles_flat = adj_tiles.reshape(slot_count, block_size, -1)
    partial_value = jnp.einsum(
        "sir,srf->sif", tiles_flat, picked, preferred_element_type=jnp.float32
    )
    alive_mask = (jnp.arange(capacity)[None, :] < send_count.reshape(owners, 1)).astype(jnp.float32)
    partial_value = (
        partial_value.reshape(owners, capacity, block_size * feat_width) * alive_mask[:, :, None]
    )
    targets = send_block.reshape(owners, capacity)
    spread = jnp.broadcast_to(targets[:, :, None], (owners, capacity, groups))
    arrived, arrived_ids = (
        lax.all_to_all(
            lax.all_to_all(partial_value, "dst", split_axis=0, concat_axis=0, tiled=True),
            "src",
            split_axis=2,
            concat_axis=1,
            tiled=True,
        ),
        lax.all_to_all(
            lax.all_to_all(spread, "dst", split_axis=0, concat_axis=0, tiled=True),
            "src",
            split_axis=2,
            concat_axis=1,
            tiled=True,
        ),
    )
    selector = (arrived_ids.reshape(1, -1) == jnp.arange(own_blocks)[:, None]).astype(jnp.float32)
    summed = jnp.dot(
        selector,
        arrived.reshape(selector.shape[1], -1),
        precision=lax.Precision.HIGHEST,
        preferred_element_type=jnp.float32,
    )
    agg_rows = summed.astype(jnp.bfloat16).reshape(-1, feat_width)
    self_rows = node_feats.reshape(-1, feat_width)
    pre_act = (
        jnp.dot(agg_rows, w_neigh, preferred_element_type=jnp.float32)
        + jnp.dot(self_rows, w_self, preferred_element_type=jnp.float32)
        + out_bias
    )
    sigmoid_z = jax.nn.sigmoid(pre_act)
    new_embed = (pre_act * sigmoid_z).astype(jnp.bfloat16).reshape(node_feats.shape)
    loss_scale = float(own_blocks * owners * block_size) ** (-0.5)
    slope = sigmoid_z * (1.0 + pre_act * (1.0 - sigmoid_z))
    grad_pre = cotangent.reshape(-1, feat_width).astype(jnp.float32) * slope * loss_scale
    grad_low = grad_pre.astype(jnp.bfloat16)
    grad_neigh = jnp.dot(agg_rows.T, grad_low, preferred_element_type=jnp.float32)
    grad_self = jnp.dot(self_rows.T, grad_low, preferred_element_type=jnp.float32)
    grad_bias = jnp.sum(grad_pre, axis=0)
    grad_neigh, grad_self, grad_bias = lax.psum((grad_neigh, grad_self, grad_bias), ("dst", "src"))
    return (new_embed, grad_neigh, grad_self, grad_bias)


def solution(mesh):
    in_specs = (
        P("dst", "src", None, None, None),
        P("dst", "src", None, None),
        P("dst", "src", None, None),
        P("dst", "src", None),
        P("dst", "src", None),
        P("dst", "src"),
        P(),
        P(),
        P(),
        P("dst", "src"),
    )
    out_specs = (P("dst", "src"), P(), P(), P())
    return jax.shard_map(
        on_device, mesh=mesh, in_specs=in_specs, out_specs=out_specs, check_vma=False
    )
```

profile of v0, /device:TPU:1, one launch (start us, length us, event | category | flops | bytes accessed | tf_op | source)
XLA Modules:
  0.0 780.6 jit_solution(10505770939572856301)
XLA Ops:
  7.2 1.4 copy.38
  8.7 0.8 copy.35
  9.5 0.7 broadcast_in_dim.5
  10.2 16.8 %all-to-all-start = ((s32[32,2,16]{2,1,0:T(2,128)}), s32[32,2,16]{2,1,0:T(2,128)S(1)}, u32[]{:S(2)}, u32[]{:S(2)}) async-start(s32[32,2,16]{2,1,0:T(2,128)} %broadcast_in_dim.5), calls=%async_computation | async-start | bytes 65536 | tf_op jit(solution)/shard_map/all_to_all | solution.py:48
  26.9 0.8 copy.39
  27.8 0.7 fusion.7
  28.5 59.7 %all-gather.2.cloned.1.call-done = bf16[64,1,8192]{2,1,0:T(2,128)(2,1)} async-done(((bf16[2,1,8192]{2,1,0:T(2,128)(2,1)}), bf16[64,1,8192]{2,1,0:T(2,128)(2,1)}) %all-gather.2.cloned.1.call-update) | async-done | bytes 1048592 | tf_op jit(solution)/shard_map/all_gather | solution.py:26
  88.3 7.9 %reduce = bf16[64,8192]{1,0:T(8,128)(2,1)S(1)} reduce(bf16[64,1,8192]{2,1,0:T(2,128)(2,1)} %all-gather.2.cloned.1.call-done, bf16[]{:T(256)} %constant.17), dimensions={1}, to_apply=%all_gather.3.reduce_sub_computation | reduce | bytes 2097154 | tf_op jit(solution)/shard_map/all_gather | solution.py:26
  96.4 13.5 %gather_fusion = bf16[512,64,128]{2,1,0:T(8,128)(2,1)} fusion(bf16[64,64,128]{2,1,0:T(8,128)(2,1)S(1)} %bitcast.38, s32[1024]{0:T(1024)S(1)} %pad_clamp_fusion), kind=kCustom, calls=%fused_computation | custom fusion | bytes 16779264 | tf_op jit(solution)/shard_map/gather | solution.py:28
  109.9 6.3 fusion.2
  116.3 2.2 reshape.102
  118.5 4.2 broadcast_multiply_fusion
  122.7 8.2 %all-to-all-start.2 = ((f32[32,2,8192]{2,1,0:T(2,128)}), f32[32,2,8192]{2,1,0:T(2,128)S(1)}, u32[]{:S(2)}, u32[]{:S(2)}) async-start(f32[32,2,8192]{2,1,0:T(2,128)} %broadcast_multiply_fusion), calls=%async_computation.2 | async-start | bytes 4194304 | tf_op jit(solution)/shard_map/all_to_all | solution.py:41
  131.0 0.7 copy.36
  131.6 97.9 %all-to-all-done.2 = f32[32,2,8192]{2,1,0:T(2,128)S(1)} async-done(((f32[32,2,8192]{2,1,0:T(2,128)}), f32[32,2,8192]{2,1,0:T(2,128)S(1)}, u32[]{:S(2)}, u32[]{:S(2)}) %all-to-all-start.2) | async-done | bytes 2097184 | tf_op jit(solution)/shard_map/all_to_all | solution.py:41
  229.6 6.4 all-to-all-start.1
  236.0 8.6 %copy.40 = f32[32,2,8192]{0,1,2:T(2,128)} copy(f32[32,2,8192]{2,1,0:T(2,128)S(1)} %all-to-all-done.2) | data formatting | bytes 4194304 | tf_op jit(solution)/shard_map/all_to_all | solution.py:41
  244.6 11.4 %reshape.117 = f32[16,1,32768]{2,1,0:T(1,128)} reshape(f32[8192,2,32]{2,1,0:T(2,128)} %bitcast.40) | data formatting | bytes 4194304
  256.0 6.8 all-to-all-start.3
  263.3 27.6 %all-to-all-done.3 = f32[16,1,32768]{2,1,0:T(1,128)S(1)} async-done(((f32[16,1,32768]{2,1,0:T(1,128)}), f32[16,1,32768]{2,1,0:T(1,128)S(1)}, u32[]{:S(2)}, u32[]{:S(2)}) %all-to-all-start.3) | async-done | bytes 2097184 | tf_op jit(solution)/shard_map/all_to_all | solution.py:40
  290.9 1.3 copy-done.1
  292.8 7.3 reduce.1
  300.1 9.2 %reshape.118 = f32[8192,2,32]{2,1,0:T(2,128)} reshape(f32[16,32768]{1,0:T(8,128)S(1)} %reduce.1) | data formatting | bytes 4194304
  309.3 10.3 %copy.41 = f32[32,2,16,512]{3,1,2,0:T(2,128)S(1)} copy(f32[32,2,16,512]{0,1,3,2:T(2,128)} %bitcast.41) | data formatting | bytes 4194304 | tf_op jit(solution)/shard_map/all_to_all | solution.py:40
  319.6 2.5 reshape.103
  322.1 2.4 convolution_convert_fusion
  324.9 0.8 convolution_bitcast_fusion
  325.7 0.8 fusion.9
  327.2 103.9 %psum.23 = f32[128]{0:T(128)} all-reduce(f32[128]{0:T(128)S(1)} %get-tuple-element.26), channel_id=1, replica_groups=mesh['dst'=32,'src'=16] {'dst','src'}, use_global_device_ids=true, to_apply=%region_3.0 | all-reduce | flops 128 | bytes 1024 | tf_op jit(solution)/shard_map/psum | solution.py:78
  431.1 339.6 %all-reduce.3.cloned.1.call-done = (f32[128,128]{1,0:T(8,128)}, f32[128,128]{0,1:T(8,128)}) async-done(((f32[128,128]{1,0:T(8,128)}, f32[128,128]{0,1:T(8,128)}), (f32[128,128]{1,0:T(8,128)}, f32[128,128]{0,1:T(8,128)})) %all-reduce.3.cloned.1.call-update) | async-done | bytes 131088 | tf_op jit(solution)/shard_map/psum | solution.py:78
  770.7 1.6 copy.42
  772.3 1.5 copy.46
  (30 shorter events, 2.4 us)
Async XLA Ops:
  7.2 317.5 %copy-start = (bf16[128,128]{1,0:T(8,128)(2,1)S(1)}, bf16[128,128]{1,0:T(8,128)(2,1)}, u32[]{:S(2)}) copy-start(bf16[128,128]{1,0:T(8,128)(2,1)} %param.17) | copy-start | bytes 98308
  7.2 81.1 %all-gather.2.cloned.1.call-start = ((), (), s32[]{:S(2)}) async-start(), calls=%async_computation.4 | async-start | bytes 2162688 | tf_op jit(solution)/shard_map/all_gather | solution.py:26
  10.2 112.5 %all-to-all-start = ((s32[32,2,16]{2,1,0:T(2,128)}), s32[32,2,16]{2,1,0:T(2,128)S(1)}, u32[]{:S(2)}, u32[]{:S(2)}) async-start(s32[32,2,16]{2,1,0:T(2,128)} %broadcast_in_dim.5), calls=%async_computation | async-start | bytes 65536 | tf_op jit(solution)/shard_map/all_to_all | solution.py:48
  122.7 106.9 %all-to-all-start.2 = ((f32[32,2,8192]{2,1,0:T(2,128)}), f32[32,2,8192]{2,1,0:T(2,128)S(1)}, u32[]{:S(2)}, u32[]{:S(2)}) async-start(f32[32,2,8192]{2,1,0:T(2,128)} %broadcast_multiply_fusion), calls=%async_computation.2 | async-start | bytes 4194304 | tf_op jit(solution)/shard_map/all_to_all | solution.py:41
  229.6 26.4 %all-to-all-start.1 = ((s32[32,2,16]{0,1,2:T(2,128)}), s32[32,2,16]{0,1,2:T(2,128)S(1)}, u32[]{:S(2)}, u32[]{:S(2)}) async-start(s32[32,2,16]{0,1,2:T(2,128)} %copy.36), calls=%async_computation.1 | async-start | bytes 32768 | tf_op jit(solution)/shard_map/all_to_all | solution.py:47
  256.0 6.9 copy-start.4
  256.0 6.9 copy-start.3
  256.0 34.9 %all-to-all-start.3 = ((f32[16,1,32768]{2,1,0:T(1,128)}), f32[16,1,32768]{2,1,0:T(1,128)S(1)}, u32[]{:S(2)}, u32[]{:S(2)}) async-start(f32[16,1,32768]{2,1,0:T(1,128)} %reshape.117), calls=%async_computation.3 | async-start | bytes 4194304 | tf_op jit(solution)/shard_map/all_to_all | solution.py:40
  262.8 507.9 %all-reduce.3.cloned.1.call-start = ((), (), s32[]{:S(2)}) async-start(), calls=%async_computation.5 | async-start | bytes 262144 | tf_op jit(solution)/shard_map/psum | solution.py:78
  290.9 1.3 copy-start.1
  322.1 2.4 copy-start.2
  322.1 2.6 copy-start.5
Sparse Core Ops, SparseCore 0:
  10.7 77.5 all-gather.1
  326.7 444.0 all-reduce.2
where the time goes:
time: 782 us; the launch traced here: 781 us
  waiting for transfers between devices  525 us (67%)
  blocking collectives  104 us (13%)
  local copies, waits for them, and re-layouts  68.5 us (9%)
  starting transfers between devices  38.3 us (5%)
  other arithmetic  20.1 us (3%)
  between operations  14.2 us (2%)
  matrix products  10.6 us (1%)
    psum x1, waiting for transfers between devices, on_device(): lax.psum((grad_neigh, grad_self, grad_bias), ('dst', 'src'))  340 us
    psum x1, blocking collectives, on_device(): lax.psum((grad_neigh, grad_self, grad_bias), ('dst', 'src'))  104 us
    all_to_all x1, waiting for transfers between devices, on_device(): lax.all_to_all(partial_value, 'dst', split_axis=0, concat_axis=0, tiled=T...  97.9 us
    all_gather x1, waiting for transfers between devices, on_device(): gathered = lax.all_gather(history, 'dst', axis=0, tiled=True)  59.7 us
    all_to_all x1, waiting for transfers between devices, on_device(): lax.all_to_all(lax.all_to_all(partial_value, 'dst', split_axis=0, concat_...  27.6 us
    unnamed x19, local copies, waits for them, and re-layouts  27.5 us
    all_to_all x1, starting transfers between devices, on_device(): lax.all_to_all(spread, 'dst', split_axis=0, concat_axis=0, tiled=True)  16.8 us
  transfers between devices with their start and end apart: 6, of which 4 were waited for; matrix products, arithmetic and copies ran while one was open for 8% of the time, Pallas kernels for 0%

commit v1 on v0

--- a/solution.py
+++ b/solution.py
@@ -75,7 +75,9 @@
     grad_neigh = jnp.dot(agg_rows.T, grad_low, preferred_element_type=jnp.float32)
     grad_self = jnp.dot(self_rows.T, grad_low, preferred_element_type=jnp.float32)
     grad_bias = jnp.sum(grad_pre, axis=0)
-    grad_neigh, grad_self, grad_bias = lax.psum((grad_neigh, grad_self, grad_bias), ("dst", "src"))
+    grad_neigh, grad_self, grad_bias = lax.psum(
+        lax.psum((grad_neigh, grad_self, grad_bias), "dst"), "src"
+    )
     return (new_embed, grad_neigh, grad_self, grad_bias)
 
 

time: 782 us -> 640 us (0.82)
  waiting for transfers between devices: 525 us -> 407 us
  blocking collectives: 104 us -> 80.2 us
    psum x1 -> x2, waiting for transfers between devices: 340 us -> 221 us  [the longest x1 191 us: on_device(): lax.psum((grad_neigh, grad_self, grad_bias), 'dst')]
    psum x1 -> x2, blocking collectives: 104 us -> 80.2 us  [the longest x1 46.1 us: on_device(): lax.psum((grad_neigh, grad_self, grad_bias), 'dst')]
  transfers between devices with their start and end apart: 6 -> 7, of which waited for: 4 -> 5; matrix products, arithmetic and copies ran while one was open for 8% -> 9% of each run, Pallas kernels for 0% -> 0%
where the time goes in v1:
time: 640 us; the launch traced here: 638 us
  waiting for transfers between devices  407 us (64%)
  blocking collectives  80.2 us (13%)
  local copies, waits for them, and re-layouts  68.4 us (11%)
  starting transfers between devices  38.4 us (6%)
  other arithmetic  20.1 us (3%)
  between operations  13.9 us (2%)
  matrix products  10.6 us (2%)
    psum x1, waiting for transfers between devices, on_device(): lax.psum((grad_neigh, grad_self, grad_bias), 'dst')  191 us
    all_to_all x1, waiting for transfers between devices, on_device(): lax.all_to_all(partial_value, 'dst', split_axis=0, concat_axis=0, tiled=T...  97.9 us
    all_gather x1, waiting for transfers between devices, on_device(): gathered = lax.all_gather(history, 'dst', axis=0, tiled=True)  59.7 us
    psum x1, blocking collectives, on_device(): lax.psum((grad_neigh, grad_self, grad_bias), 'dst')  46.1 us
    psum x1, blocking collectives, on_device(): lax.psum(lax.psum((grad_neigh, grad_self, grad_bias), 'dst'), 'src')  34.1 us
    psum x1, waiting for transfers between devices, on_device(): lax.psum(lax.psum((grad_neigh, grad_self, grad_bias), 'dst'), 'src')  30.4 us
    all_to_all x1, waiting for transfers between devices, on_device(): lax.all_to_all(lax.all_to_all(partial_value, 'dst', split_axis=0, concat_...  27.6 us
    unnamed x19, local copies, waits for them, and re-layouts  27.5 us
  transfers between devices with their start and end apart: 7, of which 5 were waited for; matrix products, arithmetic and copies ran while one was open for 9% of the time, Pallas kernels for 0%

profile of v1, /device:TPU:1, one launch (start us, length us, event | category | flops | bytes accessed | tf_op | source)
XLA Modules:
  0.0 638.3 jit_solution(12921014070610407846)
XLA Ops:
  7.2 1.4 copy.38
  8.7 0.8 copy.35
  10.2 16.8 %all-to-all-start = ((s32[32,2,16]{2,1,0:T(2,128)}), s32[32,2,16]{2,1,0:T(2,128)S(1)}, u32[]{:S(2)}, u32[]{:S(2)}) async-start(s32[32,2,16]{2,1,0:T(2,128)} %broadcast_in_dim.5), calls=%async_computation | async-start | bytes 65536 | tf_op jit(solution)/shard_map/all_to_all | solution.py:48
  26.9 0.8 copy.39
  27.8 0.7 fusion.7
  28.5 59.7 %all-gather.2.cloned.1.call-done = bf16[64,1,8192]{2,1,0:T(2,128)(2,1)} async-done(((bf16[2,1,8192]{2,1,0:T(2,128)(2,1)}), bf16[64,1,8192]{2,1,0:T(2,128)(2,1)}) %all-gather.2.cloned.1.call-update) | async-done | bytes 1048592 | tf_op jit(solution)/shard_map/all_gather | solution.py:26
  88.3 7.9 %reduce = bf16[64,8192]{1,0:T(8,128)(2,1)S(1)} reduce(bf16[64,1,8192]{2,1,0:T(2,128)(2,1)} %all-gather.2.cloned.1.call-done, bf16[]{:T(256)} %constant.17), dimensions={1}, to_apply=%all_gather.3.reduce_sub_computation | reduce | bytes 2097154 | tf_op jit(solution)/shard_map/all_gather | solution.py:26
  96.4 13.5 %gather_fusion = bf16[512,64,128]{2,1,0:T(8,128)(2,1)} fusion(bf16[64,64,128]{2,1,0:T(8,128)(2,1)S(1)} %bitcast.38, s32[1024]{0:T(1024)S(1)} %pad_clamp_fusion), kind=kCustom, calls=%fused_computation | custom fusion | bytes 16779264 | tf_op jit(solution)/shard_map/gather | solution.py:28
  109.9 6.3 fusion.2
  116.3 2.2 reshape.102
  118.5 4.2 broadcast_multiply_fusion
  122.7 8.2 %all-to-all-start.2 = ((f32[32,2,8192]{2,1,0:T(2,128)}), f32[32,2,8192]{2,1,0:T(2,128)S(1)}, u32[]{:S(2)}, u32[]{:S(2)}) async-start(f32[32,2,8192]{2,1,0:T(2,128)} %broadcast_multiply_fusion), calls=%async_computation.2 | async-start | bytes 4194304 | tf_op jit(solution)/shard_map/all_to_all | solution.py:41
  131.7 97.9 %all-to-all-done.2 = f32[32,2,8192]{2,1,0:T(2,128)S(1)} async-done(((f32[32,2,8192]{2,1,0:T(2,128)}), f32[32,2,8192]{2,1,0:T(2,128)S(1)}, u32[]{:S(2)}, u32[]{:S(2)}) %all-to-all-start.2) | async-done | bytes 2097184 | tf_op jit(solution)/shard_map/all_to_all | solution.py:41
  229.6 6.4 %all-to-all-start.1 = ((s32[32,2,16]{0,1,2:T(2,128)}), s32[32,2,16]{0,1,2:T(2,128)S(1)}, u32[]{:S(2)}, u32[]{:S(2)}) async-start(s32[32,2,16]{0,1,2:T(2,128)} %copy.36), calls=%async_computation.1 | async-start | bytes 32768 | tf_op jit(solution)/shard_map/all_to_all | solution.py:47
  236.0 8.5 %copy.40 = f32[32,2,8192]{0,1,2:T(2,128)} copy(f32[32,2,8192]{2,1,0:T(2,128)S(1)} %all-to-all-done.2) | data formatting | bytes 4194304 | tf_op jit(solution)/shard_map/all_to_all | solution.py:41
  244.5 11.4 %reshape.117 = f32[16,1,32768]{2,1,0:T(1,128)} reshape(f32[8192,2,32]{2,1,0:T(2,128)} %bitcast.40) | data formatting | bytes 4194304
  255.9 6.8 %all-to-all-start.3 = ((f32[16,1,32768]{2,1,0:T(1,128)}), f32[16,1,32768]{2,1,0:T(1,128)S(1)}, u32[]{:S(2)}, u32[]{:S(2)}) async-start(f32[16,1,32768]{2,1,0:T(1,128)} %reshape.117), calls=%async_computation.3 | async-start | bytes 4194304 | tf_op jit(solution)/shard_map/all_to_all | solution.py:40
  263.2 27.6 %all-to-all-done.3 = f32[16,1,32768]{2,1,0:T(1,128)S(1)} async-done(((f32[16,1,32768]{2,1,0:T(1,128)}), f32[16,1,32768]{2,1,0:T(1,128)S(1)}, u32[]{:S(2)}, u32[]{:S(2)}) %all-to-all-start.3) | async-done | bytes 2097184 | tf_op jit(solution)/shard_map/all_to_all | solution.py:40
  290.8 1.3 copy-done.1
  292.7 7.3 %reduce.1 = f32[16,32768]{1,0:T(8,128)S(1)} reduce(f32[16,1,32768]{2,1,0:T(1,128)} %copy-done.1, f32[]{:T(128)} %broadcast.40), dimensions={1}, to_apply=%all_to_all.33.reduce_sub_computation | reduce | bytes 4194308 | tf_op jit(solution)/shard_map/all_to_all | solution.py:40
  300.0 9.2 %reshape.118 = f32[8192,2,32]{2,1,0:T(2,128)} reshape(f32[16,32768]{1,0:T(8,128)S(1)} %reduce.1) | data formatting | bytes 4194304
  309.2 10.3 %copy.41 = f32[32,2,16,512]{3,1,2,0:T(2,128)S(1)} copy(f32[32,2,16,512]{0,1,3,2:T(2,128)} %bitcast.41) | data formatting | bytes 4194304 | tf_op jit(solution)/shard_map/all_to_all | solution.py:40
  319.6 2.5 reshape.103
  322.1 2.4 convolution_convert_fusion
  324.8 0.8 convolution_bitcast_fusion
  325.6 0.8 fusion.9
  326.5 191.0 %all-reduce.5.cloned.1.call-done = (f32[128,128]{1,0:T(8,128)}, f32[128,128]{0,1:T(8,128)}) async-done(((f32[128,128]{1,0:T(8,128)}, f32[128,128]{0,1:T(8,128)}), (f32[128,128]{1,0:T(8,128)}, f32[128,128]{0,1:T(8,128)})) %all-reduce.5.cloned.1.call-update) | async-done | bytes 131088 | tf_op jit(solution)/shard_map/psum | solution.py:79
  518.2 46.1 %psum.46 = f32[128]{0:T(128)S(1)} all-reduce(f32[128]{0:T(128)S(1)} %get-tuple-element.28), channel_id=1, replica_groups=mesh['dst'=32,'src'=16] {'dst'}, use_global_device_ids=true, to_apply=%region_5.0 | all-reduce | flops 128 | bytes 1024 | tf_op jit(solution)/shard_map/psum | solution.py:79
  564.2 34.1 %psum.47 = f32[128]{0:T(128)} all-reduce(f32[128]{0:T(128)S(1)} %psum.46), channel_id=1, replica_groups=mesh['dst'=32,'src'=16] {'src'}, use_global_device_ids=true, to_apply=%region_6.0 | all-reduce | flops 128 | bytes 1024 | tf_op jit(solution)/shard_map/psum | solution.py:78
  598.4 30.4 %all-reduce.7.cloned.1.call-done = (f32[128,128]{1,0:T(8,128)}, f32[128,128]{0,1:T(8,128)}) async-done(((f32[128,128]{1,0:T(8,128)}, f32[128,128]{0,1:T(8,128)}), (f32[128,128]{1,0:T(8,128)}, f32[128,128]{0,1:T(8,128)})) %all-reduce.7.cloned.1.call-update) | async-done | bytes 131088 | tf_op jit(solution)/shard_map/psum | solution.py:78
  628.7 1.6 copy.42
  630.3 1.5 copy.48
  (34 shorter events, 3.9 us)
Async XLA Ops:
  7.2 317.5 %copy-start = (bf16[128,128]{1,0:T(8,128)(2,1)S(1)}, bf16[128,128]{1,0:T(8,128)(2,1)}, u32[]{:S(2)}) copy-start(bf16[128,128]{1,0:T(8,128)(2,1)} %param.17) | copy-start | bytes 98308
  7.2 81.1 %all-gather.2.cloned.1.call-start = ((), (), s32[]{:S(2)}) async-start(), calls=%async_computation.4 | async-start | bytes 2162688 | tf_op jit(solution)/shard_map/all_gather | solution.py:26
  10.2 112.6 %all-to-all-start = ((s32[32,2,16]{2,1,0:T(2,128)}), s32[32,2,16]{2,1,0:T(2,128)S(1)}, u32[]{:S(2)}, u32[]{:S(2)}) async-start(s32[32,2,16]{2,1,0:T(2,128)} %broadcast_in_dim.5), calls=%async_computation | async-start | bytes 65536 | tf_op jit(solution)/shard_map/all_to_all | solution.py:48
  122.7 106.9 %all-to-all-start.2 = ((f32[32,2,8192]{2,1,0:T(2,128)}), f32[32,2,8192]{2,1,0:T(2,128)S(1)}, u32[]{:S(2)}, u32[]{:S(2)}) async-start(f32[32,2,8192]{2,1,0:T(2,128)} %broadcast_multiply_fusion), calls=%async_computation.2 | async-start | bytes 4194304 | tf_op jit(solution)/shard_map/all_to_all | solution.py:41
  229.6 26.3 %all-to-all-start.1 = ((s32[32,2,16]{0,1,2:T(2,128)}), s32[32,2,16]{0,1,2:T(2,128)S(1)}, u32[]{:S(2)}, u32[]{:S(2)}) async-start(s32[32,2,16]{0,1,2:T(2,128)} %copy.36), calls=%async_computation.1 | async-start | bytes 32768 | tf_op jit(solution)/shard_map/all_to_all | solution.py:47
  255.9 6.9 %copy-start.4 = (bf16[16,512]{1,0:T(8,128)(2,1)S(1)}, bf16[16,512]{1,0:T(8,128)(2,1)}, u32[]{:S(2)}) copy-start(bf16[16,512]{1,0:T(8,128)(2,1)} %param.15) | copy-start | bytes 49156
  255.9 6.9 %copy-start.3 = (bf16[16,512]{1,0:T(8,128)(2,1)S(1)}, bf16[16,512]{1,0:T(8,128)(2,1)}, u32[]{:S(2)}) copy-start(bf16[16,512]{1,0:T(8,128)(2,1)} %param.19) | copy-start | bytes 49156
  255.9 34.9 %all-to-all-start.3 = ((f32[16,1,32768]{2,1,0:T(1,128)}), f32[16,1,32768]{2,1,0:T(1,128)S(1)}, u32[]{:S(2)}, u32[]{:S(2)}) async-start(f32[16,1,32768]{2,1,0:T(1,128)} %reshape.117), calls=%async_computation.3 | async-start | bytes 4194304 | tf_op jit(solution)/shard_map/all_to_all | solution.py:40
  262.7 254.8 %all-reduce.5.cloned.1.call-start = ((), (), s32[]{:S(2)}) async-start(), calls=%async_computation.5 | async-start | bytes 262144 | tf_op jit(solution)/shard_map/psum | solution.py:79
  290.8 1.3 copy-start.1
  322.1 2.4 copy-start.2
  322.1 2.6 copy-start.5
  326.5 302.3 %all-reduce.7.cloned.1.call-start = ((), (), s32[]{:S(2)}) async-start(), calls=%async_computation.6 | async-start | bytes 262144 | tf_op jit(solution)/shard_map/psum | solution.py:78
Sparse Core Ops, SparseCore 0:
  10.7 77.5 all-gather.1
  326.6 190.8 all-reduce.4
  521.1 107.5 all-reduce.6
